TPU v7x, 256 devices: a whole 4x4x8 slice. The times are simulated.
256 devices in a mesh: dp: 4 (over y), sx: 4 (over x_lo, core), sy: 16 (over z, x_hi).
Axes of the slice: x: 4 (x_hi: 2, x_lo: 2; x = x_hi * 2 + x_lo), y: 4, z: 8, core: 2. Of those that a mesh axis runs over, the one named last changes fastest.
Arguments:
- features: bfloat16 [4, 4, 16, 3072, 128], P('dp', 'sx', 'sy'), may hold values from -6 to 6
- cotangent: bfloat16 [4, 4, 16, 3072, 128], P('dp', 'sx', 'sy'), may hold values from -6 to 6
- weights: bfloat16 [27, 128, 128], replicated, may hold values from -0.109375 to 0.109375
- tables: int32 [4, 4, 16, 27, 24], P('dp', 'sx', 'sy'), may hold values from 0 to 56, as said below
- send_lists: int32 [4, 4, 16, 4], P('dp', 'sx', 'sy'), may hold values from 0 to 23, as said below
- counts: int32 [4, 4, 16], P('dp', 'sx', 'sy'), may hold values from 6 to 24, as said below
Outputs:
- output: bfloat16 [4, 4, 16, 3072, 128], P('dp', 'sx', 'sy')
- input_grad: bfloat16 [4, 4, 16, 3072, 128], P('dp', 'sx', 'sy')
- weight_grad: float32 [27, 128, 128], replicated
Inputs may be any that keep to these rules, and one draw needn't show every extreme that they name: `tables`: entries below 24 name a block of the tile, 24 + n * 4 + s' the s'-th sent block of neighbour direction n, 56 the empty block; under offset 27 // 2 every block reads itself. `send_lists`: the 4 blocks of one tile are distinct. `counts`: some tile has all 24 blocks active.
All inputs are finite; a program needn't handle non-finite values.
Results may differ from a plain program's by a relative error of at most 0.001.
Values may be sent and summed in bfloat16 or wider, within the bound.
A program may use at most 64 MiB of HBM per device.

v0:
```python
import math
import jax
import jax.numpy as jnp
from jax import lax
from jax.sharding import PartitionSpec as P

directions = ((-1, -1), (-1, 0), (-1, 1), (0, -1), (0, 1), (1, -1), (1, 0), (1, 1))


def shifted(block, axis, distance):
    devices = range(lax.axis_size(axis))
    route = [(i - distance, i) for i in devices if i - distance in devices]
    return lax.ppermute(block, axis, route)


def padded(cells, sides, width):
    for axis, dim in sides:
        count = lax.axis_size(axis)
        ends = count - 1
        head = lax.slice_in_dim(cells, 0, width, axis=dim)
        tail = lax.slice_in_dim(cells, cells.shape[dim] - width, cells.shape[dim], axis=dim)
        cells = jnp.concatenate(
            [
                lax.ppermute(tail, axis, [(i, (i + 1) % count) for i in range(ends)]),
                cells,
                lax.ppermute(head, axis, [((i + 1) % count, i) for i in range(ends)]),
            ],
            axis=dim,
        )
    return cells


def local(features, cotangent, weights, tables, send_lists, counts):
    num_blocks = tables.shape[4]
    num_sent = send_lists.shape[3]
    offsets = weights.shape[0]
    channels = weights.shape[1]
    width_block = features.shape[3] // num_blocks
    group_size = 4
    active = (jnp.arange(num_blocks) < counts.reshape(())).astype(jnp.bfloat16)[:, None, None]
    active_full = active.astype(jnp.float32)
    blocks_in = features.reshape(num_blocks, width_block, channels) * active
    blocks_grad = cotangent.reshape(num_blocks, width_block, channels) * active
    offset_table = tables.reshape(offsets, num_blocks)
    sent_ids = send_lists.reshape(num_sent)
    groups = jnp.arange(num_blocks // group_size)

    def grad_group(accum, group):
        start = group * group_size
        picks = lax.dynamic_slice_in_dim(offset_table, start, group_size, 1)
        grad_rows = lax.dynamic_slice_in_dim(blocks_grad, start, group_size, 0)
        contrib = jnp.einsum(
            "gvd,kcd->kgvc", grad_rows, weights, preferred_element_type=jnp.float32
        )
        accum = accum.at[picks.reshape(-1)].add(
            contrib.reshape(offsets * group_size, width_block, channels)
        )
        return (accum, None)

    num_ext = num_blocks + 8 * num_sent + 1
    grad_ext, unused_rows = lax.scan(
        grad_group, jnp.zeros((num_ext, width_block, channels), jnp.float32), groups
    )
    halo_grads = grad_ext[num_blocks : num_blocks + 8 * num_sent].reshape(
        8, num_sent * width_block, channels
    )
    received = jnp.zeros((num_sent * width_block, channels), jnp.float32)
    for slot_index, (step_x, step_y) in enumerate(directions):
        portion = halo_grads[slot_index]
        if step_x != 0:
            portion = shifted(portion, "sx", step_x)
        if step_y != 0:
            portion = shifted(portion, "sy", step_y)
        received = received + portion
    local_grad = (
        grad_ext[:num_blocks].at[sent_ids].add(received.reshape(num_sent, width_block, channels))
    )
    input_grad = (local_grad * active_full).astype(jnp.bfloat16).reshape(features.shape)
    outgoing = blocks_in[sent_ids].reshape(1, 1, num_sent * width_block, channels)
    bordered = padded(outgoing, (("sx", 0), ("sy", 1)), 1)
    neighbours = [
        bordered[1 + step_x, 1 + step_y].reshape(num_sent, width_block, channels)
        for step_x, step_y in directions
    ]
    extended = jnp.concatenate(
        [blocks_in] + neighbours + [jnp.zeros((1, width_block, channels), jnp.bfloat16)], axis=0
    )

    def forward_group(accum, group):
        start = group * group_size
        picks = lax.dynamic_slice_in_dim(offset_table, start, group_size, 1)
        gathered = extended[picks]
        grad_rows = lax.dynamic_slice_in_dim(blocks_grad, start, group_size, 0)
        rows_active = lax.dynamic_slice_in_dim(active_full, start, group_size, 0)
        outputs = jnp.einsum("kgvc,kcd->gvd", gathered, weights, preferred_element_type=jnp.float32)
        accum = accum + jnp.einsum(
            "kgvc,gvd->kcd", gathered, grad_rows, preferred_element_type=jnp.float32
        )
        return (accum, (outputs * rows_active).astype(jnp.bfloat16))

    weight_part, outputs = lax.scan(
        forward_group, jnp.zeros((offsets, channels, channels), jnp.float32), groups
    )
    output = outputs.reshape(features.shape)
    total = (
        num_blocks * width_block * lax.axis_size("dp") * lax.axis_size("sx") * lax.axis_size("sy")
    )
    scaled_part = weight_part * (1.0 / math.sqrt(total))
    weight_grad = lax.psum(scaled_part, ("dp", "sx", "sy"))
    return (output, input_grad, weight_grad)


def solution(mesh):
    return jax.shard_map(
        local,
        mesh=mesh,
        in_specs=(
            P("dp", "sx", "sy", None, None),
            P("dp", "sx", "sy", None, None),
            P(),
            P("dp", "sx", "sy", None, None),
            P("dp", "sx", "sy", None),
            P("dp", "sx", "sy"),
        ),
        out_specs=(P("dp", "sx", "sy", None, None), P("dp", "sx", "sy", None, None), P()),
        check_vma=False,
    )
```

profile of v0, /device:TPU:2, one launch (start us, length us, event | category | flops | bytes accessed | tf_op | source)
XLA Modules:
  0.0 617.5 jit_solution(9292657915912878841)
XLA Ops:
  8.5 3.2 constant_dynamic-update-slice_fusion.9
  12.3 1.9 collective-permute-start.1
  14.3 2.4 collective-permute-start
  17.4 2.4 broadcast_in_dim.26
  19.8 184.4 %while.23 = (s32[]{:T(128)}, f32[57,128,128]{2,1,0:T(8,128)}, s32[6]{0:T(128)S(1)}, s32[27,24]{1,0:T(8,128)}, bf16[24,128,128]{2,1,0:T(8,128)(2,1)}, /*index=5*/...) while((s32[]{:T(128)}, f32[57,128,128]{2,1,0:T(8,128)}, s32[6]{0:T(128)S(1)}, ...), condition=%wide.region_4.5_spmd, body=%wide.region_2.0_spmd.sunk | while | flops 454754624 | bytes 43486336 | solution.py:61
  21.9 2.3 convolution_bitcast_fusion.3
  24.3 3.3 copy.22
  27.6 22.9 %scatter_fusion = f32[57,128,128]{2,1,0:T(8,128)} fusion(f32[57,128,128]{2,1,0:T(8,128)} %get-tuple-element.307, s32[108]{0:T(128)S(1)} %fusion.33, f32[108,128,128]{2,1,0:T(8,128)} %bitcast.107), kind=kCustom, calls=%fused_computation.2.clone.1 | custom fusion | flops 1769472 | bytes 21234096 | tf_op jit(solution)/shard_map/while/body/eval_jaxpr/scatter-add | solution.py:55
  52.6 2.3 convolution_bitcast_fusion.3
  55.0 3.3 copy.22
  58.3 22.9 %scatter_fusion = f32[57,128,128]{2,1,0:T(8,128)} fusion(f32[57,128,128]{2,1,0:T(8,128)} %get-tuple-element.307, s32[108]{0:T(128)S(1)} %fusion.33, f32[108,128,128]{2,1,0:T(8,128)} %bitcast.107), kind=kCustom, calls=%fused_computation.2.clone.1 | custom fusion | flops 1769472 | bytes 21234096 | tf_op jit(solution)/shard_map/while/body/eval_jaxpr/scatter-add | solution.py:55
  83.4 2.3 convolution_bitcast_fusion.3
  85.7 3.3 copy.22
  89.1 22.8 %scatter_fusion = f32[57,128,128]{2,1,0:T(8,128)} fusion(f32[57,128,128]{2,1,0:T(8,128)} %get-tuple-element.307, s32[108]{0:T(128)S(1)} %fusion.33, f32[108,128,128]{2,1,0:T(8,128)} %bitcast.107), kind=kCustom, calls=%fused_computation.2.clone.1 | custom fusion | flops 1769472 | bytes 21234096 | tf_op jit(solution)/shard_map/while/body/eval_jaxpr/scatter-add | solution.py:55
  114.0 2.3 convolution_bitcast_fusion.3
  116.4 3.3 copy.22
  119.7 23.0 %scatter_fusion = f32[57,128,128]{2,1,0:T(8,128)} fusion(f32[57,128,128]{2,1,0:T(8,128)} %get-tuple-element.307, s32[108]{0:T(128)S(1)} %fusion.33, f32[108,128,128]{2,1,0:T(8,128)} %bitcast.107), kind=kCustom, calls=%fused_computation.2.clone.1 | custom fusion | flops 1769472 | bytes 21234096 | tf_op jit(solution)/shard_map/while/body/eval_jaxpr/scatter-add | solution.py:55
  144.9 2.3 convolution_bitcast_fusion.3
  147.2 3.3 copy.22
  150.6 22.9 %scatter_fusion = f32[57,128,128]{2,1,0:T(8,128)} fusion(f32[57,128,128]{2,1,0:T(8,128)} %get-tuple-element.307, s32[108]{0:T(128)S(1)} %fusion.33, f32[108,128,128]{2,1,0:T(8,128)} %bitcast.107), kind=kCustom, calls=%fused_computation.2.clone.1 | custom fusion | flops 1769472 | bytes 21234096 | tf_op jit(solution)/shard_map/while/body/eval_jaxpr/scatter-add | solution.py:55
  175.6 2.3 convolution_bitcast_fusion.3
  177.9 3.3 copy.22
  181.3 22.9 %scatter_fusion = f32[57,128,128]{2,1,0:T(8,128)} fusion(f32[57,128,128]{2,1,0:T(8,128)} %get-tuple-element.307, s32[108]{0:T(128)S(1)} %fusion.33, f32[108,128,128]{2,1,0:T(8,128)} %bitcast.107), kind=kCustom, calls=%fused_computation.2.clone.1 | custom fusion | flops 1769472 | bytes 21234096 | tf_op jit(solution)/shard_map/while/body/eval_jaxpr/scatter-add | solution.py:55
  204.3 4.3 collective-permute-start.2
  208.6 2.9 fusion.17
  211.4 1.9 collective-permute-start.14
  213.4 3.6 collective-permute-start.6
  217.0 1.9 collective-permute-start.13
  218.9 1.9 collective-permute-start.11
  220.9 1.3 collective-permute-start.3
  223.6 10.0 %collective-permute-done.3 = bf16[3,1,512,128]{3,2,1,0:T(8,128)(2,1)S(1)} collective-permute-done((bf16[3,1,512,128]{3,2,1,0:T(8,128)(2,1)S(1)}, bf16[3,1,512,128]{3,2,1,0:T(8,128)(2,1)S(1)}, u32[]{:S(2)}, u32[]{:S(2)}) %collective-permute-start.3) | collective-permute-done | bytes 393248 | tf_op jit(solution)/shard_map/ppermute | solution.py:26
  233.5 6.1 collective-permute-start.10
  244.8 79.9 %while.24 = (s32[]{:T(128)}, f32[27,128,128]{2,1,0:T(8,128)}, bf16[6,4,128,128]{3,2,1,0:T(8,128)(2,1)}, s32[6]{0:T(128)}, s32[27,24]{1,0:T(8,128)}, /*index=5*/b...) while((s32[]{:T(128)}, f32[27,128,128]{2,1,0:T(8,128)}, ...), condition=%wide.region_1.0_spmd.clone, body=%wide.region_0.1_spmd.clone.sunk | while | flops 906986816 | bytes 33004880 | solution.py:101
  248.2 2.7 gather_fusion
  251.0 3.0 fusion.39
  254.0 2.9 bitcast_add_fusion.2
  261.5 2.7 gather_fusion
  264.3 3.0 fusion.39
  267.3 2.9 bitcast_add_fusion.2
  274.8 2.7 gather_fusion
  277.6 3.0 fusion.39
  280.6 2.9 bitcast_add_fusion.2
  288.1 2.7 gather_fusion
  290.9 3.0 fusion.39
  294.0 2.9 bitcast_add_fusion.2
  301.5 2.7 gather_fusion
  304.2 3.0 fusion.39
  307.3 2.9 bitcast_add_fusion.2
  314.8 2.7 gather_fusion
  317.5 3.0 fusion.39
  320.6 2.9 bitcast_add_fusion.2
  324.7 4.2 collective-permute-start.7
  328.9 4.3 collective-permute-start.4
  333.2 3.0 broadcast_multiply_fusion
  336.2 1.3 collective-permute-start.9
  337.5 6.1 collective-permute-start.15
  343.6 1.3 collective-permute-start.12
  344.9 6.1 collective-permute-start.8
  351.0 1.3 collective-permute-start.5
  352.3 1.5 slice.68
  353.8 9.3 %collective-permute-done.15 = f32[512,128]{1,0:T(8,128)S(1)} collective-permute-done((f32[512,128]{1,0:T(8,128)}, f32[512,128]{1,0:T(8,128)S(1)}, u32[]{:S(2)}, u32[]{:S(2)}) %collective-permute-start.15) | collective-permute-done | bytes 262176 | tf_op jit(solution)/shard_map/ppermute | solution.py:13
  363.1 5.7 collective-permute-done.8
  371.9 235.9 %all-reduce.2.cloned.1.call-done = f32[27,128,128]{2,1,0:T(8,128)} async-done(((f32[27,128,128]{2,1,0:T(8,128)}), f32[27,128,128]{2,1,0:T(8,128)}) %all-reduce.2.cloned.1.call-update) | async-done | bytes 1769488 | tf_op jit(solution)/shard_map/psum | solution.py:109
  607.8 2.9 copy.52
  (122 shorter events, 44.4 us)
Async XLA Ops:
  7.2 600.6 %all-reduce.2.cloned.1.call-start = ((), (), s32[]{:S(2)}) async-start(), calls=%async_computation | async-start | bytes 3538944 | tf_op jit(solution)/shard_map/psum | solution.py:109
  8.5 8.2 %copy-start.3 = (s32[1,1,1,27,24]{3,4,2,1,0:T(8,128)S(1)}, s32[1,1,1,27,24]{3,4,2,1,0:T(8,128)}, u32[]{:S(2)}) copy-start(s32[1,1,1,27,24]{3,4,2,1,0:T(8,128)} %param.13) | copy-start | bytes 7780
  12.3 191.9 %collective-permute-start.1 = (bf16[1,1,512,128]{3,2,1,0:T(8,128)(2,1)S(1)}, bf16[1,1,512,128]{3,2,1,0:T(8,128)(2,1)S(1)}, u32[]{:S(2)}, u32[]{:S(2)}) collective-permute-start(bf16[1,1,512,128]{3,2,1,0:T(8,128)(2,1)S(1)} %bitcast.116), channel_id=1, source_target_pairs={{16,0},{32,16},{48,32},{17,1},{33,17},{49,33},{18,2},{34,18},{50,3... | collective-permute-start | bytes 393224 | tf_op jit(solution)/shard_map/ppermute | solution.py:26
  14.3 189.9 %collective-permute-start = (bf16[1,1,512,128]{3,2,1,0:T(8,128)(2,1)S(1)}, bf16[1,1,512,128]{3,2,1,0:T(8,128)(2,1)S(1)}, u32[]{:S(2)}, u32[]{:S(2)}) collective-permute-start(bf16[1,1,512,128]{3,2,1,0:T(8,128)(2,1)S(1)} %bitcast.117), channel_id=1, source_target_pairs={{0,16},{16,32},{32,48},{1,17},{17,33},{33,49},{2,18},{18,34},{34,5... | collective-permute-start | bytes 393224 | tf_op jit(solution)/shard_map/ppermute | solution.py:24
  204.3 16.7 %collective-permute-start.2 = (bf16[3,1,512,128]{3,2,1,0:T(8,128)(2,1)S(1)}, bf16[3,1,512,128]{3,2,1,0:T(8,128)(2,1)S(1)}, u32[]{:S(2)}, u32[]{:S(2)}) collective-permute-start(bf16[3,1,512,128]{3,2,1,0:T(8,128)(2,1)S(1)} %pad_maximum_fusion), channel_id=1, source_target_pairs={{0,1},{1,2},{2,3},{3,4},{4,5},{5,6},{6,7},{7,8},{8,9},{9,10},{10,1... | collective-permute-start | bytes 1179656 | tf_op jit(solution)/shard_map/ppermute | solution.py:24
  211.4 113.2 %collective-permute-start.14 = (f32[512,128]{1,0:T(8,128)}, f32[512,128]{1,0:T(8,128)}, u32[]{:S(2)}, u32[]{:S(2)}) collective-permute-start(f32[512,128]{1,0:T(8,128)} %bitcast.30), channel_id=1, source_target_pairs={{0,16},{16,32},{32,48},{1,17},{17,33},{33,49},{2,18},{18,34},{34,5... | collective-permute-start | bytes 786440 | tf_op jit(solution)/shard_map/ppermute | solution.py:13
  213.4 115.5 %collective-permute-start.6 = (f32[512,128]{1,0:T(8,128)}, f32[512,128]{1,0:T(8,128)}, u32[]{:S(2)}, u32[]{:S(2)}) collective-permute-start(f32[512,128]{1,0:T(8,128)} %bitcast.24), channel_id=1, source_target_pairs={{16,0},{32,16},{48,32},{17,1},{33,17},{49,33},{18,2},{34,18},{50,3... | collective-permute-start | bytes 786440 | tf_op jit(solution)/shard_map/ppermute | solution.py:13
  217.0 119.1 %collective-permute-start.13 = (f32[512,128]{1,0:T(8,128)}, f32[512,128]{1,0:T(8,128)}, u32[]{:S(2)}, u32[]{:S(2)}) collective-permute-start(f32[512,128]{1,0:T(8,128)} %bitcast.29), channel_id=1, source_target_pairs={{0,16},{16,32},{32,48},{1,17},{17,33},{33,49},{2,18},{18,34},{34,5... | collective-permute-start | bytes 786440 | tf_op jit(solution)/shard_map/ppermute | solution.py:13
  218.9 118.5 %collective-permute-start.11 = (f32[512,128]{1,0:T(8,128)}, f32[512,128]{1,0:T(8,128)}, u32[]{:S(2)}, u32[]{:S(2)}) collective-permute-start(f32[512,128]{1,0:T(8,128)} %bitcast.28), channel_id=1, source_target_pairs={{0,16},{16,32},{32,48},{1,17},{17,33},{33,49},{2,18},{18,34},{34,5... | collective-permute-start | bytes 786440 | tf_op jit(solution)/shard_map/ppermute | solution.py:13
  220.9 12.6 %collective-permute-start.3 = (bf16[3,1,512,128]{3,2,1,0:T(8,128)(2,1)S(1)}, bf16[3,1,512,128]{3,2,1,0:T(8,128)(2,1)S(1)}, u32[]{:S(2)}, u32[]{:S(2)}) collective-permute-start(bf16[3,1,512,128]{3,2,1,0:T(8,128)(2,1)S(1)} %pad_maximum_fusion), channel_id=1, source_target_pairs={{1,0},{2,1},{3,2},{4,3},{5,4},{6,5},{7,6},{8,7},{9,8},{10,9},{11,1... | collective-permute-start | bytes 1179656 | tf_op jit(solution)/shard_map/ppermute | solution.py:26
  233.5 110.0 %collective-permute-start.10 = (f32[512,128]{1,0:T(8,128)}, f32[512,128]{1,0:T(8,128)}, u32[]{:S(2)}, u32[]{:S(2)}) collective-permute-start(f32[512,128]{1,0:T(8,128)} %bitcast.27), channel_id=1, source_target_pairs={{0,1},{1,2},{2,3},{3,4},{4,5},{5,6},{6,7},{7,8},{8,9},{9,10},{10,1... | collective-permute-start | bytes 786440 | tf_op jit(solution)/shard_map/ppermute | solution.py:13
  250.9 3.1 copy-start
  256.9 1.2 copy-start.1
  264.3 3.1 copy-start
  270.2 1.2 copy-start.1
  277.6 3.1 copy-start
  283.5 1.2 copy-start.1
  290.9 3.1 copy-start
  296.8 1.2 copy-start.1
  304.2 3.1 copy-start
  310.2 1.2 copy-start.1
  317.5 3.1 copy-start
  323.5 1.2 copy-start.1
  324.7 20.2 %collective-permute-start.7 = (f32[512,128]{1,0:T(8,128)}, f32[512,128]{1,0:T(8,128)S(1)}, u32[]{:S(2)}, u32[]{:S(2)}) collective-permute-start(f32[512,128]{1,0:T(8,128)} %bitcast.127), channel_id=1, source_target_pairs={{16,0},{32,16},{48,32},{17,1},{33,17},{49,33},{18,2},{34,18},{50,3... | collective-permute-start | bytes 786440 | tf_op jit(solution)/shard_map/ppermute | solution.py:13
  328.9 22.1 %collective-permute-start.4 = (f32[512,128]{1,0:T(8,128)}, f32[512,128]{1,0:T(8,128)S(1)}, u32[]{:S(2)}, u32[]{:S(2)}) collective-permute-start(f32[512,128]{1,0:T(8,128)} %bitcast.126), channel_id=1, source_target_pairs={{16,0},{32,16},{48,32},{17,1},{33,17},{49,33},{18,2},{34,18},{50,3... | collective-permute-start | bytes 786440 | tf_op jit(solution)/shard_map/ppermute | solution.py:13
  333.2 3.0 copy-start.2
  336.2 17.6 %collective-permute-start.9 = (f32[512,128]{1,0:T(8,128)S(1)}, f32[512,128]{1,0:T(8,128)S(1)}, u32[]{:S(2)}, u32[]{:S(2)}) collective-permute-start(f32[512,128]{1,0:T(8,128)S(1)} %bitcast.125), channel_id=1, source_target_pairs={{1,0},{2,1},{3,2},{4,3},{5,4},{6,5},{7,6},{8,7},{9,8},{10,9},{11,1... | collective-permute-start | bytes 786440 | tf_op jit(solution)/shard_map/ppermute | solution.py:13
  337.5 25.6 %collective-permute-start.15 = (f32[512,128]{1,0:T(8,128)}, f32[512,128]{1,0:T(8,128)S(1)}, u32[]{:S(2)}, u32[]{:S(2)}) collective-permute-start(f32[512,128]{1,0:T(8,128)} %collective-permute-done.14), channel_id=1, source_target_pairs={{0,1},{1,2},{2,3},{3,4},{4,5},{5,6},{6,7},{7,8},{8,9},{9,10},{10,1... | collective-permute-start | bytes 786440 | tf_op jit(solution)/shard_map/ppermute | solution.py:13
  343.6 19.5 %collective-permute-start.12 = (f32[512,128]{1,0:T(8,128)}, f32[512,128]{1,0:T(8,128)S(1)}, u32[]{:S(2)}, u32[]{:S(2)}) collective-permute-start(f32[512,128]{1,0:T(8,128)} %collective-permute-done.11), channel_id=1, source_target_pairs={{1,0},{2,1},{3,2},{4,3},{5,4},{6,5},{7,6},{8,7},{9,8},{10,9},{11,1... | collective-permute-start | bytes 786440 | tf_op jit(solution)/shard_map/ppermute | solution.py:13
  344.9 23.9 %collective-permute-start.8 = (f32[512,128]{1,0:T(8,128)S(1)}, f32[512,128]{1,0:T(8,128)S(1)}, u32[]{:S(2)}, u32[]{:S(2)}) collective-permute-start(f32[512,128]{1,0:T(8,128)S(1)} %collective-permute-done.7), channel_id=1, source_target_pairs={{0,1},{1,2},{2,3},{3,4},{4,5},{5,6},{6,7},{7,8},{8,9},{9,10},{10,1... | collective-permute-start | bytes 786440 | tf_op jit(solution)/shard_map/ppermute | solution.py:13
  351.0 17.8 %collective-permute-start.5 = (f32[512,128]{1,0:T(8,128)S(1)}, f32[512,128]{1,0:T(8,128)S(1)}, u32[]{:S(2)}, u32[]{:S(2)}) collective-permute-start(f32[512,128]{1,0:T(8,128)S(1)} %collective-permute-done.4), channel_id=1, source_target_pairs={{1,0},{2,1},{3,2},{4,3},{5,4},{6,5},{7,6},{8,7},{9,8},{10,9},{11,1... | collective-permute-start | bytes 786440 | tf_op jit(solution)/shard_map/ppermute | solution.py:13
Sparse Core Ops, SparseCore 0:
  336.3 271.4 all-reduce.1
where the time goes:
time: 621 us; the launch traced here: 618 us
  waiting for transfers between devices  261 us (42%)
  other arithmetic  152 us (24%)
  local copies, waits for them, and re-layouts  81.9 us (13%)
  starting transfers between devices  49.9 us (8%)
  matrix products  49.6 us (8%)
  between operations  15 us (2%)
  loops' own time  7.98 us (1%)
    psum x1, waiting for transfers between devices, local(): weight_grad = lax.psum(scaled_part, ('dp', 'sx', 'sy'))  236 us
    scatter-add x6, other arithmetic, grad_group(): accum.at[picks.reshape(-1)]  137 us
    ppermute x12, starting transfers between devices, shifted(): return lax.ppermute(block, axis, route)  39.9 us
    transpose x6, local copies, waits for them, and re-layouts, grad_group(): jnp.einsum('gvd,kcd->kgvc', grad_rows, weights, preferred_element_type=jn...  20.1 us
    dot_general x6, matrix products, forward_group(): jnp.einsum('kgvc,kcd->gvd', gathered, weights, preferred_element_type=jnp...  18.2 us
    dot_general x6, matrix products, forward_group(): jnp.einsum('kgvc,gvd->kcd', gathered, grad_rows, preferred_element_type=j...  17.3 us
    gather x6, local copies, waits for them, and re-layouts, forward_group(): gathered = extended[picks]  16.4 us
    ppermute x12, waiting for transfers between devices, shifted(): return lax.ppermute(block, axis, route)  15 us
  transfers between devices with their start and end apart: 17, of which 4 were waited for; matrix products, arithmetic and copies ran while one was open for 44% of the time, Pallas kernels for 0%

commit v1 on v0

--- a/solution.py
+++ b/solution.py
@@ -106,7 +106,9 @@
         num_blocks * width_block * lax.axis_size("dp") * lax.axis_size("sx") * lax.axis_size("sy")
     )
     scaled_part = weight_part * (1.0 / math.sqrt(total))
-    weight_grad = lax.psum(scaled_part, ("dp", "sx", "sy"))
+    weight_grad = scaled_part
+    for d in (("sx", "sy"), "dp"):
+        weight_grad = lax.psum(weight_grad, d)
     return (output, input_grad, weight_grad)
 
 

time: 621 us -> 576 us (0.928)
  waiting for transfers between devices: 261 us -> 223 us
    psum x1 -> x2, waiting for transfers between devices: 236 us -> 192 us  [local(): weight_grad = lax.psum(weight_grad, d)]
    ppermute x2, waiting for transfers between devices: 0.01 us -> 16.5 us  [padded(): lax.ppermute(tail, axis, [(i, (i + 1) % count) for i in range(ends)])]
    ppermute x2, waiting for transfers between devices: 9.99 us -> 0.08 us  [padded(): lax.ppermute(head, axis, [((i + 1) % count, i) for i in range(ends)])]
  transfers between devices with their start and end apart: 17 -> 18, of which waited for: 4 -> 7; matrix products, arithmetic and copies ran while one was open for 44% -> 33% of each run, Pallas kernels for 0% -> 0%
where the time goes in v1:
time: 576 us; the launch traced here: 571 us
  waiting for transfers between devices  223 us (39%)
  other arithmetic  151 us (26%)
  local copies, waits for them, and re-layouts  81 us (14%)
  matrix products  47.6 us (8%)
  starting transfers between devices  44.8 us (8%)
  between operations  15 us (3%)
  loops' own time  8.06 us (1%)
    psum x2, waiting for transfers between devices, local(): weight_grad = lax.psum(weight_grad, d)  192 us
    scatter-add x6, other arithmetic, grad_group(): accum.at[picks.reshape(-1)]  138 us
    ppermute x12, starting transfers between devices, shifted(): return lax.ppermute(block, axis, route)  35.4 us
    transpose x6, local copies, waits for them, and re-layouts, grad_group(): jnp.einsum('gvd,kcd->kgvc', grad_rows, weights, preferred_element_type=jn...  20.1 us
    dot_general x6, matrix products, forward_group(): jnp.einsum('kgvc,kcd->gvd', gathered, weights, preferred_element_type=jnp...  18.2 us
    dot_general x6, matrix products, forward_group(): jnp.einsum('kgvc,gvd->kcd', gathered, grad_rows, preferred_element_type=j...  17.4 us
    ppermute x2, waiting for transfers between devices, padded(): lax.ppermute(tail, axis, [(i, (i + 1) % count) for i in range(ends)])  16.5 us
    gather x6, local copies, waits for them, and re-layouts, forward_group(): gathered = extended[picks]  16.4 us
  transfers between devices with their start and end apart: 18, of which 7 were waited for; matrix products, arithmetic and copies ran while one was open for 33% of the time, Pallas kernels for 0%

profile of v1, /device:TPU:2, one launch (start us, length us, event | category | flops | bytes accessed | tf_op | source)
XLA Modules:
  0.0 570.6 jit_solution(6021334607917595484)
XLA Ops:
  8.5 3.2 constant_dynamic-update-slice_fusion.9
  12.3 1.9 collective-permute-start.1
  14.3 2.4 collective-permute-start
  16.8 4.4 collective-permute-done
  21.2 3.7 collective-permute-start.2
  26.9 12.1 %collective-permute-done.2 = bf16[3,1,512,128]{3,2,1,0:T(8,128)(2,1)S(1)} collective-permute-done((bf16[3,1,512,128]{3,2,1,0:T(8,128)(2,1)S(1)}, bf16[3,1,512,128]{3,2,1,0:T(8,128)(2,1)S(1)}, u32[]{:S(2)}, u32[]{:S(2)}) %collective-permute-start.2) | collective-permute-done | bytes 393248 | tf_op jit(solution)/shard_map/ppermute | solution.py:24
  45.5 80.3 %while.24 = (s32[]{:T(128)}, f32[27,128,128]{2,1,0:T(8,128)}, bf16[6,4,128,128]{3,2,1,0:T(8,128)(2,1)}, s32[6]{0:T(128)}, s32[27,24]{1,0:T(8,128)}, /*index=5*/b...) while((s32[]{:T(128)}, f32[27,128,128]{2,1,0:T(8,128)}, ...), condition=%wide.region_1.0_spmd.clone, body=%wide.region_0.1_spmd.clone.sunk | while | flops 906986816 | bytes 33004880 | solution.py:101
  49.0 2.7 gather_fusion
  51.8 3.0 fusion.39
  54.8 2.9 bitcast_add_fusion.2
  62.4 2.7 gather_fusion
  65.2 3.0 fusion.39
  68.2 2.9 bitcast_add_fusion.2
  72.3 1.3 dynamic_slice.52
  75.8 2.7 gather_fusion
  78.6 3.0 fusion.39
  81.6 2.9 bitcast_add_fusion.2
  85.7 1.3 dynamic_slice.52
  89.2 2.7 gather_fusion
  91.9 3.0 fusion.39
  95.0 2.9 bitcast_add_fusion.2
  102.6 2.7 gather_fusion
  105.3 3.0 fusion.39
  108.4 2.9 bitcast_add_fusion.2
  116.0 2.7 gather_fusion
  118.7 3.0 fusion.39
  121.8 2.9 bitcast_add_fusion.2
  125.9 2.9 broadcast_multiply_fusion
  128.9 191.7 %all-reduce.3.cloned.1.call-done = f32[27,128,128]{2,1,0:T(8,128)} async-done(((f32[27,128,128]{2,1,0:T(8,128)}), f32[27,128,128]{2,1,0:T(8,128)}) %all-reduce.3.cloned.1.call-update) | async-done | bytes 1769488 | tf_op jit(solution)/shard_map/psum | solution.py:111
  320.7 2.4 broadcast_in_dim.26
  323.1 182.7 %while.23 = (s32[]{:T(128)}, f32[57,128,128]{2,1,0:T(8,128)}, s32[6]{0:T(128)S(1)}, s32[27,24]{1,0:T(8,128)}, bf16[24,128,128]{2,1,0:T(8,128)(2,1)}, /*index=5*/...) while((s32[]{:T(128)}, f32[57,128,128]{2,1,0:T(8,128)}, s32[6]{0:T(128)S(1)}, ...), condition=%wide.region_4.5_spmd, body=%wide.region_2.0_spmd.sunk | while | flops 454754624 | bytes 43486336 | solution.py:61
  325.2 2.0 convolution_bitcast_fusion.3
  327.2 3.3 copy.22
  330.6 23.0 %scatter_fusion = f32[57,128,128]{2,1,0:T(8,128)} fusion(f32[57,128,128]{2,1,0:T(8,128)} %get-tuple-element.307, s32[108]{0:T(128)S(1)} %fusion.33, f32[108,128,128]{2,1,0:T(8,128)} %bitcast.107), kind=kCustom, calls=%fused_computation.2.clone.1 | custom fusion | flops 1769472 | bytes 21234096 | tf_op jit(solution)/shard_map/while/body/eval_jaxpr/scatter-add | solution.py:55
  355.7 2.0 convolution_bitcast_fusion.3
  357.7 3.3 copy.22
  361.1 23.1 %scatter_fusion = f32[57,128,128]{2,1,0:T(8,128)} fusion(f32[57,128,128]{2,1,0:T(8,128)} %get-tuple-element.307, s32[108]{0:T(128)S(1)} %fusion.33, f32[108,128,128]{2,1,0:T(8,128)} %bitcast.107), kind=kCustom, calls=%fused_computation.2.clone.1 | custom fusion | flops 1769472 | bytes 21234096 | tf_op jit(solution)/shard_map/while/body/eval_jaxpr/scatter-add | solution.py:55
  386.3 2.0 convolution_bitcast_fusion.3
  388.3 3.3 copy.22
  391.7 22.8 %scatter_fusion = f32[57,128,128]{2,1,0:T(8,128)} fusion(f32[57,128,128]{2,1,0:T(8,128)} %get-tuple-element.307, s32[108]{0:T(128)S(1)} %fusion.33, f32[108,128,128]{2,1,0:T(8,128)} %bitcast.107), kind=kCustom, calls=%fused_computation.2.clone.1 | custom fusion | flops 1769472 | bytes 21234096 | tf_op jit(solution)/shard_map/while/body/eval_jaxpr/scatter-add | solution.py:55
  416.6 2.0 convolution_bitcast_fusion.3
  418.6 3.3 copy.22
  422.0 23.0 %scatter_fusion = f32[57,128,128]{2,1,0:T(8,128)} fusion(f32[57,128,128]{2,1,0:T(8,128)} %get-tuple-element.307, s32[108]{0:T(128)S(1)} %fusion.33, f32[108,128,128]{2,1,0:T(8,128)} %bitcast.107), kind=kCustom, calls=%fused_computation.2.clone.1 | custom fusion | flops 1769472 | bytes 21234096 | tf_op jit(solution)/shard_map/while/body/eval_jaxpr/scatter-add | solution.py:55
  447.1 2.0 convolution_bitcast_fusion.3
  449.1 3.3 copy.22
  452.5 22.9 %scatter_fusion = f32[57,128,128]{2,1,0:T(8,128)} fusion(f32[57,128,128]{2,1,0:T(8,128)} %get-tuple-element.307, s32[108]{0:T(128)S(1)} %fusion.33, f32[108,128,128]{2,1,0:T(8,128)} %bitcast.107), kind=kCustom, calls=%fused_computation.2.clone.1 | custom fusion | flops 1769472 | bytes 21234096 | tf_op jit(solution)/shard_map/while/body/eval_jaxpr/scatter-add | solution.py:55
  477.5 2.0 convolution_bitcast_fusion.3
  479.5 3.3 copy.22
  482.8 22.9 %scatter_fusion = f32[57,128,128]{2,1,0:T(8,128)} fusion(f32[57,128,128]{2,1,0:T(8,128)} %get-tuple-element.307, s32[108]{0:T(128)S(1)} %fusion.33, f32[108,128,128]{2,1,0:T(8,128)} %bitcast.107), kind=kCustom, calls=%fused_computation.2.clone.1 | custom fusion | flops 1769472 | bytes 21234096 | tf_op jit(solution)/shard_map/while/body/eval_jaxpr/scatter-add | solution.py:55
  505.8 1.6 fusion.17
  507.4 1.9 collective-permute-start.14
  509.4 3.6 collective-permute-start.6
  513.0 1.9 collective-permute-start.13
  514.9 1.9 collective-permute-start.11
  516.9 3.4 collective-permute-start.10
  520.2 4.0 collective-permute-start.7
  524.2 2.7 collective-permute-start.4
  528.3 6.1 %collective-permute-start.15 = (f32[512,128]{1,0:T(8,128)S(1)}, f32[512,128]{1,0:T(8,128)S(1)}, u32[]{:S(2)}, u32[]{:S(2)}) collective-permute-start(f32[512,128]{1,0:T(8,128)S(1)} %collective-permute-done.14), channel_id=1, source_target_pairs={{0,1},{1,2},{2,3},{3,4},{4,5},{5,6},{6,7},{7,8},{8,9},{9,10},{10,1... | collective-permute-start | bytes 786440 | tf_op jit(solution)/shard_map/ppermute | solution.py:13
  535.7 6.1 %collective-permute-start.8 = (f32[512,128]{1,0:T(8,128)S(1)}, f32[512,128]{1,0:T(8,128)S(1)}, u32[]{:S(2)}, u32[]{:S(2)}) collective-permute-start(f32[512,128]{1,0:T(8,128)S(1)} %collective-permute-done.7), channel_id=1, source_target_pairs={{0,1},{1,2},{2,3},{3,4},{4,5},{5,6},{6,7},{7,8},{8,9},{9,10},{10,1... | collective-permute-start | bytes 786440 | tf_op jit(solution)/shard_map/ppermute | solution.py:13
  541.7 1.6 collective-permute-done.4
  544.6 1.5 slice.68
  546.1 8.6 %collective-permute-done.15 = f32[512,128]{1,0:T(8,128)S(1)} collective-permute-done((f32[512,128]{1,0:T(8,128)S(1)}, f32[512,128]{1,0:T(8,128)S(1)}, u32[]{:S(2)}, u32[]{:S(2)}) %collective-permute-start.15) | collective-permute-done | bytes 262176 | tf_op jit(solution)/shard_map/ppermute | solution.py:13
  554.7 4.3 collective-permute-done.8
  560.9 2.9 copy.53
  (125 shorter events, 46.3 us)
Async XLA Ops:
  7.2 313.5 %all-reduce.3.cloned.1.call-start = ((), (), s32[]{:S(2)}) async-start(), calls=%async_computation | async-start | bytes 3538944 | tf_op jit(solution)/shard_map/psum | solution.py:111
  8.5 16.4 %copy-start.3 = (s32[1,1,1,27,24]{3,4,2,1,0:T(8,128)S(1)}, s32[1,1,1,27,24]{3,4,2,1,0:T(8,128)}, u32[]{:S(2)}) copy-start(s32[1,1,1,27,24]{3,4,2,1,0:T(8,128)} %param.13) | copy-start | bytes 7780
  12.3 4.4 collective-permute-start.1
  14.3 6.9 %collective-permute-start = (bf16[1,1,512,128]{3,2,1,0:T(8,128)(2,1)S(1)}, bf16[1,1,512,128]{3,2,1,0:T(8,128)(2,1)S(1)}, u32[]{:S(2)}, u32[]{:S(2)}) collective-permute-start(bf16[1,1,512,128]{3,2,1,0:T(8,128)(2,1)S(1)} %bitcast.120), channel_id=1, source_target_pairs={{0,16},{16,32},{32,48},{1,17},{17,33},{33,49},{2,18},{18,34},{34,5... | collective-permute-start | bytes 393224 | tf_op jit(solution)/shard_map/ppermute | solution.py:24
  21.2 17.8 %collective-permute-start.2 = (bf16[3,1,512,128]{3,2,1,0:T(8,128)(2,1)S(1)}, bf16[3,1,512,128]{3,2,1,0:T(8,128)(2,1)S(1)}, u32[]{:S(2)}, u32[]{:S(2)}) collective-permute-start(bf16[3,1,512,128]{3,2,1,0:T(8,128)(2,1)S(1)} %pad_maximum_fusion), channel_id=1, source_target_pairs={{0,1},{1,2},{2,3},{3,4},{4,5},{5,6},{6,7},{7,8},{8,9},{9,10},{10,1... | collective-permute-start | bytes 1179656 | tf_op jit(solution)/shard_map/ppermute | solution.py:24
  25.6 14.7 %collective-permute-start.3 = (bf16[3,1,512,128]{3,2,1,0:T(8,128)(2,1)S(1)}, bf16[3,1,512,128]{3,2,1,0:T(8,128)(2,1)S(1)}, u32[]{:S(2)}, u32[]{:S(2)}) collective-permute-start(bf16[3,1,512,128]{3,2,1,0:T(8,128)(2,1)S(1)} %pad_maximum_fusion), channel_id=1, source_target_pairs={{1,0},{2,1},{3,2},{4,3},{5,4},{6,5},{7,6},{8,7},{9,8},{10,9},{11,1... | collective-permute-start | bytes 1179656 | tf_op jit(solution)/shard_map/ppermute | solution.py:26
  51.8 3.1 copy-start
  57.7 1.2 copy-start.1
  65.2 3.1 copy-start
  71.1 1.2 copy-start.1
  78.5 3.1 copy-start
  84.5 1.2 copy-start.1
  91.9 3.1 copy-start
  97.9 1.2 copy-start.1
  105.3 3.1 copy-start
  111.3 1.2 copy-start.1
  118.7 3.1 copy-start
  124.7 1.2 copy-start.1
  128.8 432.1 %all-reduce.5.cloned.1.call-start = ((), (), s32[]{:S(2)}) async-start(), calls=%async_computation.1 | async-start | bytes 3538944 | tf_op jit(solution)/shard_map/psum | solution.py:111
  320.7 2.4 copy-start.2
  507.4 12.8 %collective-permute-start.14 = (f32[512,128]{1,0:T(8,128)S(1)}, f32[512,128]{1,0:T(8,128)S(1)}, u32[]{:S(2)}, u32[]{:S(2)}) collective-permute-start(f32[512,128]{1,0:T(8,128)S(1)} %bitcast.132), channel_id=1, source_target_pairs={{0,16},{16,32},{32,48},{1,17},{17,33},{33,49},{2,18},{18,34},{34,5... | collective-permute-start | bytes 786440 | tf_op jit(solution)/shard_map/ppermute | solution.py:13
  509.4 14.9 %collective-permute-start.6 = (f32[512,128]{1,0:T(8,128)S(1)}, f32[512,128]{1,0:T(8,128)S(1)}, u32[]{:S(2)}, u32[]{:S(2)}) collective-permute-start(f32[512,128]{1,0:T(8,128)S(1)} %bitcast.131), channel_id=1, source_target_pairs={{16,0},{32,16},{48,32},{17,1},{33,17},{49,33},{18,2},{34,18},{50,3... | collective-permute-start | bytes 786440 | tf_op jit(solution)/shard_map/ppermute | solution.py:13
  513.0 13.9 %collective-permute-start.13 = (f32[512,128]{1,0:T(8,128)S(1)}, f32[512,128]{1,0:T(8,128)S(1)}, u32[]{:S(2)}, u32[]{:S(2)}) collective-permute-start(f32[512,128]{1,0:T(8,128)S(1)} %bitcast.130), channel_id=1, source_target_pairs={{0,16},{16,32},{32,48},{1,17},{17,33},{33,49},{2,18},{18,34},{34,5... | collective-permute-start | bytes 786440 | tf_op jit(solution)/shard_map/ppermute | solution.py:13
  514.9 13.3 %collective-permute-start.11 = (f32[512,128]{1,0:T(8,128)S(1)}, f32[512,128]{1,0:T(8,128)S(1)}, u32[]{:S(2)}, u32[]{:S(2)}) collective-permute-start(f32[512,128]{1,0:T(8,128)S(1)} %bitcast.129), channel_id=1, source_target_pairs={{0,16},{16,32},{32,48},{1,17},{17,33},{33,49},{2,18},{18,34},{34,5... | collective-permute-start | bytes 786440 | tf_op jit(solution)/shard_map/ppermute | solution.py:13
  516.9 17.5 %collective-permute-start.10 = (f32[512,128]{1,0:T(8,128)S(1)}, f32[512,128]{1,0:T(8,128)S(1)}, u32[]{:S(2)}, u32[]{:S(2)}) collective-permute-start(f32[512,128]{1,0:T(8,128)S(1)} %bitcast.128), channel_id=1, source_target_pairs={{0,1},{1,2},{2,3},{3,4},{4,5},{5,6},{6,7},{7,8},{8,9},{9,10},{10,1... | collective-permute-start | bytes 786440 | tf_op jit(solution)/shard_map/ppermute | solution.py:13
  520.2 15.4 %collective-permute-start.7 = (f32[512,128]{1,0:T(8,128)S(1)}, f32[512,128]{1,0:T(8,128)S(1)}, u32[]{:S(2)}, u32[]{:S(2)}) collective-permute-start(f32[512,128]{1,0:T(8,128)S(1)} %bitcast.127), channel_id=1, source_target_pairs={{16,0},{32,16},{48,32},{17,1},{33,17},{49,33},{18,2},{34,18},{50,3... | collective-permute-start | bytes 786440 | tf_op jit(solution)/shard_map/ppermute | solution.py:13
  524.2 19.1 %collective-permute-start.4 = (f32[512,128]{1,0:T(8,128)S(1)}, f32[512,128]{1,0:T(8,128)S(1)}, u32[]{:S(2)}, u32[]{:S(2)}) collective-permute-start(f32[512,128]{1,0:T(8,128)S(1)} %bitcast.126), channel_id=1, source_target_pairs={{16,0},{32,16},{48,32},{17,1},{33,17},{49,33},{18,2},{34,18},{50,3... | collective-permute-start | bytes 786440 | tf_op jit(solution)/shard_map/ppermute | solution.py:13
  526.9 19.2 %collective-permute-start.9 = (f32[512,128]{1,0:T(8,128)S(1)}, f32[512,128]{1,0:T(8,128)S(1)}, u32[]{:S(2)}, u32[]{:S(2)}) collective-permute-start(f32[512,128]{1,0:T(8,128)S(1)} %bitcast.125), channel_id=1, source_target_pairs={{1,0},{2,1},{3,2},{4,3},{5,4},{6,5},{7,6},{8,7},{9,8},{10,9},{11,1... | collective-permute-start | bytes 786440 | tf_op jit(solution)/shard_map/ppermute | solution.py:13
  528.3 26.4 %collective-permute-start.15 = (f32[512,128]{1,0:T(8,128)S(1)}, f32[512,128]{1,0:T(8,128)S(1)}, u32[]{:S(2)}, u32[]{:S(2)}) collective-permute-start(f32[512,128]{1,0:T(8,128)S(1)} %collective-permute-done.14), channel_id=1, source_target_pairs={{0,1},{1,2},{2,3},{3,4},{4,5},{5,6},{6,7},{7,8},{8,9},{9,10},{10,1... | collective-permute-start | bytes 786440 | tf_op jit(solution)/shard_map/ppermute | solution.py:13
  534.3 20.3 %collective-permute-start.12 = (f32[512,128]{1,0:T(8,128)S(1)}, f32[512,128]{1,0:T(8,128)S(1)}, u32[]{:S(2)}, u32[]{:S(2)}) collective-permute-start(f32[512,128]{1,0:T(8,128)S(1)} %collective-permute-done.11), channel_id=1, source_target_pairs={{1,0},{2,1},{3,2},{4,3},{5,4},{6,5},{7,6},{8,7},{9,8},{10,9},{11,1... | collective-permute-start | bytes 786440 | tf_op jit(solution)/shard_map/ppermute | solution.py:13
  535.7 23.3 %collective-permute-start.8 = (f32[512,128]{1,0:T(8,128)S(1)}, f32[512,128]{1,0:T(8,128)S(1)}, u32[]{:S(2)}, u32[]{:S(2)}) collective-permute-start(f32[512,128]{1,0:T(8,128)S(1)} %collective-permute-done.7), channel_id=1, source_target_pairs={{0,1},{1,2},{2,3},{3,4},{4,5},{5,6},{6,7},{7,8},{8,9},{9,10},{10,1... | collective-permute-start | bytes 786440 | tf_op jit(solution)/shard_map/ppermute | solution.py:13
  543.3 15.7 %collective-permute-start.5 = (f32[512,128]{1,0:T(8,128)S(1)}, f32[512,128]{1,0:T(8,128)S(1)}, u32[]{:S(2)}, u32[]{:S(2)}) collective-permute-start(f32[512,128]{1,0:T(8,128)S(1)} %collective-permute-done.4), channel_id=1, source_target_pairs={{1,0},{2,1},{3,2},{4,3},{5,4},{6,5},{7,6},{8,7},{9,8},{10,9},{11,1... | collective-permute-start | bytes 786440 | tf_op jit(solution)/shard_map/ppermute | solution.py:13
Sparse Core Ops, SparseCore 0:
  128.9 191.6 all-reduce.2
  323.0 57.5 all-reduce.4
